TPU v7x, 32 devices: a whole 2x2x4 slice. The times are simulated.
32 devices in a mesh: groups: 2 (over y), freq: 16 (over z, x, core).
Axes of the slice: x: 2, y: 2, z: 4, core: 2. Of those that a mesh axis runs over, the one named last changes fastest.
Arguments:
- refl: bfloat16 [128, 2, 512, 512], P(('groups', 'freq')), parts along dimension 0, may hold values from -0.1875 to 0.1875
- refl_scale: float32 [128, 4], P(('groups', 'freq')), parts along dimension 0, may hold values from 0.5 to 4
- freq_index: int32 [128], P(('groups', 'freq')), parts along dimension 0, may hold values from 1 to 1023, as said below
- fd_plus: bfloat16 [4096, 32, 512], P(('groups', 'freq')), parts along dimension 0, may hold values from -6 to 6
- onset: int32 [32768], P(('groups', 'freq')), parts along dimension 0, may hold values from 128 to 767
Outputs:
- f_minus: bfloat16 [4096, 32, 512], P(('groups', 'freq')), parts along dimension 0
- f_plus: float32 [4096, 32, 512], P(('groups', 'freq')), parts along dimension 0
There are 2 independent parts, one for each index of `groups`. A program takes and returns all parts, laid end to end along the dimension named above; each array names one. Nothing has to cross between parts.
Inputs may be any that keep to these rules, and one draw needn't show every extreme that they name: `freq_index`: the bins are distinct and ascending; the first is 1 and the last is 1023.
All inputs are finite; a program needn't handle non-finite values.
Results may differ from a plain program's by a relative error of at most 0.01.
Values may be sent and summed in bfloat16 or wider, within the bound.
No kernel may reach another device: no remote copies, remote signals or barrier semaphores. Data moves between devices by JAX's collectives and lax.ppermute only.
A program may use at most 128 MiB of HBM per device.

v0:
```python
import math
import jax
import jax.numpy as jnp
from jax import lax
from jax.sharding import PartitionSpec as P


def to_columns(field):
    return lax.all_to_all(field, "freq", split_axis=1, concat_axis=0, tiled=True)


def to_time(field):
    return lax.all_to_all(field, "freq", split_axis=0, concat_axis=1, tiled=True)


def local(refl, refl_scale, freq_index, fd_plus, onset):
    nfreq_dev = refl.shape[0]
    nrec = refl.shape[2]
    t_dev, points, _ = fd_plus.shape
    columns = points * nrec
    nshard = lax.axis_size("freq")
    ntime = t_dev * nshard
    width = columns // nshard
    first_col = lax.axis_index("freq") * width
    bins, scales = (
        lax.all_gather(freq_index, "freq", axis=0, tiled=True),
        lax.all_gather(refl_scale, "freq", axis=0, tiled=True),
    )
    nblocks = scales.shape[1]
    times = jnp.arange(ntime, dtype=jnp.int32)
    phase = bins[:, None] * times[None, :] % ntime
    angle = phase.astype(jnp.float32) * jnp.float32(2.0 * math.pi / ntime)
    cosine = jnp.cos(angle).astype(jnp.bfloat16)
    sine = jnp.sin(angle).astype(jnp.bfloat16)
    col_ids = first_col + jnp.arange(width, dtype=jnp.int32)
    block_ids = col_ids % nrec // (nrec // nblocks)
    onehot = (block_ids[None, :] == jnp.arange(nblocks, dtype=jnp.int32)[:, None]).astype(
        jnp.float32
    )
    col_scale = jnp.dot(
        scales, onehot, precision=lax.Precision.HIGHEST, preferred_element_type=jnp.float32
    )
    signed = jnp.where(times < ntime // 2, times, times - ntime)
    keep = (jnp.abs(signed)[:, None] < onset[None, :]).astype(jnp.float32)
    contract_time = (((0,), (0,)), ((), ()))

    def forward(colfield, table_c, table_s):
        real = jnp.dot(table_c, colfield, preferred_element_type=jnp.float32)
        imag = -jnp.dot(table_s, colfield, preferred_element_type=jnp.float32)
        spectrum = jnp.stack(
            [(real * col_scale).astype(jnp.bfloat16), (imag * col_scale).astype(jnp.bfloat16)],
            axis=1,
        )
        return lax.all_to_all(spectrum, "freq", split_axis=0, concat_axis=2, tiled=True)

    def convolve(spectrum, sign):
        spectrum = spectrum.reshape(nfreq_dev, 2, points, nrec)
        spec_r = spectrum[:, 0]
        spec_i = spectrum[:, 1]
        resp_r = refl[:, 0]
        resp_i = refl[:, 1]

        def apply(resp, spec):
            return jnp.einsum("frs,fvs->fvr", resp, spec, preferred_element_type=jnp.float32)

        out_r = apply(resp_r, spec_r) - sign * apply(resp_i, spec_i)
        out_i = apply(resp_r, spec_i) + sign * apply(resp_i, spec_r)
        stacked = jnp.stack([out_r.astype(jnp.bfloat16), out_i.astype(jnp.bfloat16)], axis=1)
        return lax.all_to_all(
            stacked.reshape(nfreq_dev, 2, columns), "freq", split_axis=2, concat_axis=0, tiled=True
        )

    def inverse(spectrum):
        trace = lax.dot_general(
            cosine, spectrum[:, 0], contract_time, preferred_element_type=jnp.float32
        )
        trace = trace - lax.dot_general(
            sine, spectrum[:, 1], contract_time, preferred_element_type=jnp.float32
        )
        return (trace * jnp.float32(2.0 / ntime) * keep).astype(jnp.bfloat16)

    direct = fd_plus.reshape(t_dev, columns)
    minus_cols = inverse(convolve(forward(to_columns(direct), cosine, sine), 1.0))
    minus_time = to_time(minus_cols)
    update_cols = inverse(convolve(forward(minus_cols, cosine, sine), -1.0))
    plus_time = direct.astype(jnp.float32) + to_time(update_cols).astype(jnp.float32)
    return (minus_time.reshape(t_dev, points, nrec), plus_time.reshape(t_dev, points, nrec))


def solution(mesh):
    return jax.shard_map(
        local,
        mesh=mesh,
        in_specs=(
            P(("groups", "freq"), None, None, None),
            P(("groups", "freq"), None),
            P(("groups", "freq")),
            P(("groups", "freq"), None, None),
            P(("groups", "freq")),
        ),
        out_specs=(P(("groups", "freq"), None, None), P(("groups", "freq"), None, None)),
        check_vma=False,
    )
```

profile of v0, /device:TPU:11, one launch (start us, length us, event | category | flops | bytes accessed | tf_op | source)
XLA Modules:
  0.0 541.2 jit_solution(8030469073627968279)
XLA Ops:
  0.6 7.9 %copy.51 = bf16[128,32,512]{0,2,1:T(8,128)(2,1)} copy(bf16[128,32,512]{2,1,0:T(8,128)(2,1)} %param.8) | data formatting | bytes 8388608 | tf_op args[3]
  8.5 6.7 %all-to-all-start = ((bf16[128,16,1024]{0,2,1:T(8,128)(2,1)}), bf16[128,16,1024]{0,2,1:T(8,128)(2,1)}, u32[]{:S(2)}, u32[]{:S(2)}) async-start(bf16[128,16,1024]{0,2,1:T(8,128)(2,1)} %bitcast.126), calls=%async_computation | async-start | bytes 8388608 | tf_op jit(solution)/shard_map/all_to_all | solution.py:9
  16.7 88.9 %all-reduce = s32[64]{0:T(128)S(1)} all-reduce(s32[64]{0:T(128)S(1)} %dynamic-update-slice), channel_id=1, replica_groups=mesh['groups'=2,'freq'=16] {'freq'}, use_global_device_ids=true, to_apply=%add | all-reduce | flops 64 | bytes 512
  105.6 18.6 %all-gather = f32[16,4,4]{2,1,0:T(4,128)S(1)} all-gather(f32[1,4,4]{2,1,0:T(4,128)S(1)} %bitcast.140), channel_id=1, replica_groups=mesh['groups'=2,'freq'=16] {'freq'}, dimensions={0}, use_global_device_ids=true | all-gather | bytes 1088 | tf_op jit(solution)/shard_map/all_gather | solution.py:27
  124.5 6.4 %copy.52 = bf16[16,128,1024]{2,1,0:T(8,128)(2,1)} copy(bf16[16,128,1024]{1,2,0:T(8,128)(2,1)} %bitcast.2) | data formatting | bytes 8388608 | tf_op jit(solution)/shard_map/all_to_all | solution.py:9
  130.9 4.5 fusion.64
  138.2 15.2 %all_to_all.114 = bf16[64,2,1024]{2,1,0:T(2,128)(2,1)S(1)} all-to-all(bf16[64,2,1024]{2,1,0:T(2,128)(2,1)S(1)} %copy.53), channel_id=1, replica_groups=mesh['groups'=2,'freq'=16] {'freq'}, dimensions={0} | all-to-all | bytes 524288 | tf_op jit(solution)/shard_map/all_to_all | solution.py:54
  161.9 13.0 %copy.57 = bf16[4,2,16384]{0,1,2:T(2,128)(2,1)} copy(bf16[4,2,16384]{2,0,1:T(4,128)(2,1)S(1)} %pad_maximum_fusion.1) | data formatting | bytes 524288 | tf_op jit(solution)/shard_map/stack | solution.py:68
  174.9 16.8 %reshape.93 = bf16[16,2,4096]{2,1,0:T(2,128)(2,1)} reshape(bf16[16384,2,4]{2,1,0:T(2,128)(2,1)} %bitcast.122) | data formatting | bytes 524288
  191.7 6.1 %all-to-all-start.2 = ((bf16[16,2,4096]{2,1,0:T(2,128)(2,1)}), bf16[16,2,4096]{2,1,0:T(2,128)(2,1)S(1)}, u32[]{:S(2)}, u32[]{:S(2)}) async-start(bf16[16,2,4096]{2,1,0:T(2,128)(2,1)} %reshape.93), calls=%async_computation.2 | async-start | bytes 524288 | tf_op jit(solution)/shard_map/all_to_all | solution.py:69
  197.8 7.9 %all-to-all-done.2 = bf16[16,2,4096]{2,1,0:T(2,128)(2,1)S(1)} async-done(((bf16[16,2,4096]{2,1,0:T(2,128)(2,1)}), bf16[16,2,4096]{2,1,0:T(2,128)(2,1)S(1)}, u32[]{:S(2)}, u32[]{:S(2)}) %all-to-all-start.2) | async-done | bytes 262176 | tf_op jit(solution)/shard_map/all_to_all | solution.py:69
  205.7 19.0 %reshape.94 = bf16[16384,2,4]{2,1,0:T(2,128)(2,1)} reshape(bf16[16,2,4096]{2,1,0:T(2,128)(2,1)S(1)} %all-to-all-done.2) | data formatting | bytes 524288
  224.7 11.9 %copy.67 = bf16[4,2,16,1024]{3,2,1,0:T(8,128)(2,1)S(1)} copy(bf16[4,2,16,1024]{0,1,3,2:T(2,128)(2,1)} %bitcast.123) | data formatting | bytes 524288 | tf_op jit(solution)/shard_map/all_to_all | solution.py:69
  240.4 4.1 fusion
  249.9 13.0 %all_to_all.115 = bf16[64,2,1024]{2,1,0:T(2,128)(2,1)S(1)} all-to-all(bf16[64,2,1024]{2,1,0:T(2,128)(2,1)S(1)} %copy.61), channel_id=1, replica_groups=mesh['groups'=2,'freq'=16] {'freq'}, dimensions={0} | all-to-all | bytes 524288 | tf_op jit(solution)/shard_map/all_to_all | solution.py:54
  271.4 13.0 %copy.63 = bf16[4,2,16384]{0,1,2:T(2,128)(2,1)} copy(bf16[4,2,16384]{2,0,1:T(4,128)(2,1)S(1)} %pad_maximum_fusion.3) | data formatting | bytes 524288 | tf_op jit(solution)/shard_map/stack | solution.py:68
  284.4 16.2 %reshape.95 = bf16[16,2,4096]{2,1,0:T(2,128)(2,1)S(1)} reshape(bf16[16384,2,4]{2,1,0:T(2,128)(2,1)} %bitcast.124) | data formatting | bytes 524288
  300.6 12.8 %all_to_all.116 = bf16[16,2,4096]{2,1,0:T(2,128)(2,1)S(1)} all-to-all(bf16[16,2,4096]{2,1,0:T(2,128)(2,1)S(1)} %reshape.95), channel_id=1, replica_groups=mesh['groups'=2,'freq'=16] {'freq'}, dimensions={0} | all-to-all | bytes 524288 | tf_op jit(solution)/shard_map/all_to_all | solution.py:69
  313.4 6.5 %all-to-all-start.3 = ((bf16[16,128,1024]{2,1,0:T(8,128)(2,1)}), bf16[16,128,1024]{2,1,0:T(8,128)(2,1)}, u32[]{:S(2)}, u32[]{:S(2)}) async-start(bf16[16,128,1024]{2,1,0:T(8,128)(2,1)} %bitcast.127), calls=%async_computation.3 | async-start | bytes 8388608 | tf_op jit(solution)/shard_map/all_to_all | solution.py:13
  319.9 19.1 %reshape.96 = bf16[16384,2,4]{2,1,0:T(2,128)(2,1)} reshape(bf16[16,2,4096]{2,1,0:T(2,128)(2,1)S(1)} %all_to_all.116) | data formatting | bytes 524288
  338.9 11.9 %copy.68 = bf16[4,2,16,1024]{3,2,1,0:T(8,128)(2,1)S(1)} copy(bf16[4,2,16,1024]{0,1,3,2:T(2,128)(2,1)} %bitcast.125) | data formatting | bytes 524288 | tf_op jit(solution)/shard_map/all_to_all | solution.py:69
  351.5 3.1 fusion.72
  354.6 4.9 fusion.1
  359.5 52.8 %all-to-all-done.3 = bf16[16,128,1024]{2,1,0:T(8,128)(2,1)} async-done(((bf16[16,128,1024]{2,1,0:T(8,128)(2,1)}), bf16[16,128,1024]{2,1,0:T(8,128)(2,1)}, u32[]{:S(2)}, u32[]{:S(2)}) %all-to-all-start.3) | async-done | bytes 4194336 | tf_op jit(solution)/shard_map/all_to_all | solution.py:13
  412.4 5.2 all-to-all-start.6
  417.6 6.5 %copy.60 = bf16[128,16,1024]{2,1,0:T(8,128)(2,1)} copy(bf16[128,16,1024]{2,0,1:T(8,128)(2,1)} %bitcast.19) | data formatting | bytes 8388608 | tf_op jit(solution)/shard_map/all_to_all | solution.py:13
  424.1 7.1 %reshape.83 = bf16[128,32,512]{2,1,0:T(8,128)(2,1)} reshape(bf16[128,16,1024]{2,1,0:T(8,128)(2,1)} %copy.60) | data formatting | bytes 8388608 | tf_op jit(solution)/shard_map/reshape | solution.py:87
  431.2 78.7 %all-to-all-done.6 = bf16[16,128,1024]{2,1,0:T(8,128)(2,1)} async-done(((bf16[16,128,1024]{2,1,0:T(8,128)(2,1)}), bf16[16,128,1024]{2,1,0:T(8,128)(2,1)}, u32[]{:S(2)}, u32[]{:S(2)}) %all-to-all-start.6) | async-done | bytes 4194336 | tf_op jit(solution)/shard_map/all_to_all | solution.py:13
  509.9 3.2 convert_bitcast_fusion
  513.2 8.3 %copy.66 = f32[128,16,1024]{2,1,0:T(8,128)} copy(f32[128,16,1024]{2,0,1:T(8,128)S(1)} %convert_bitcast_fusion) | data formatting | bytes 16777216 | tf_op jit(solution)/shard_map/convert_element_type | solution.py:86
  521.4 9.3 %reshape.85 = f32[128,32,512]{2,1,0:T(8,128)} reshape(f32[128,16,1024]{2,1,0:T(8,128)} %copy.66) | data formatting | bytes 16777216 | tf_op jit(solution)/shard_map/convert_element_type | solution.py:86
  530.7 10.2 %convert_add_fusion = f32[128,32,512]{2,1,0:T(8,128)} fusion(f32[128,32,512]{2,1,0:T(8,128)} %reshape.85, bf16[128,32,512]{2,1,0:T(8,128)(2,1)} %param.8), kind=kLoop, calls=%fused_computation.5 | loop fusion | flops 4194304 | bytes 20971520 | tf_op jit(solution)/shard_map/add | solution.py:86
  (53 shorter events, 30.4 us)
Async XLA Ops:
  8.5 6.7 %copy-start.7 = (u32[32]{0:T(128)S(1)}, u32[32]{0:T(128)}, u32[]{:S(2)}) copy-start(u32[32]{0:T(128)} %constant.68) | copy-start | bytes 388
  8.5 8.0 %copy-start.6 = (s32[4]{0:T(128)S(1)}, s32[4]{0:T(128)}, u32[]{:S(2)}) copy-start(s32[4]{0:T(128)} %param.7) | copy-start | bytes 52
  8.5 97.1 %copy-start.4 = (f32[4,4]{1,0:T(4,128)S(1)}, f32[4,4]{1,0:T(4,128)}, u32[]{:S(2)}) copy-start(f32[4,4]{1,0:T(4,128)} %param.6) | copy-start | bytes 196
  8.5 115.9 %all-to-all-start = ((bf16[128,16,1024]{0,2,1:T(8,128)(2,1)}), bf16[128,16,1024]{0,2,1:T(8,128)(2,1)}, u32[]{:S(2)}, u32[]{:S(2)}) async-start(bf16[128,16,1024]{0,2,1:T(8,128)(2,1)} %bitcast.126), calls=%async_computation | async-start | bytes 8388608 | tf_op jit(solution)/shard_map/all_to_all | solution.py:9
  130.9 4.5 copy-start.3
  153.7 4.8 copy-start
  191.7 14.0 %all-to-all-start.2 = ((bf16[16,2,4096]{2,1,0:T(2,128)(2,1)}), bf16[16,2,4096]{2,1,0:T(2,128)(2,1)S(1)}, u32[]{:S(2)}, u32[]{:S(2)}) async-start(bf16[16,2,4096]{2,1,0:T(2,128)(2,1)} %reshape.93), calls=%async_computation.2 | async-start | bytes 524288 | tf_op jit(solution)/shard_map/all_to_all | solution.py:69
  237.3 3.1 copy-start.5
  244.5 5.1 copy-start.2
  263.2 4.8 copy-start.1
  313.4 99.0 %all-to-all-start.3 = ((bf16[16,128,1024]{2,1,0:T(8,128)(2,1)}), bf16[16,128,1024]{2,1,0:T(8,128)(2,1)}, u32[]{:S(2)}, u32[]{:S(2)}) async-start(bf16[16,128,1024]{2,1,0:T(8,128)(2,1)} %bitcast.127), calls=%async_computation.3 | async-start | bytes 8388608 | tf_op jit(solution)/shard_map/all_to_all | solution.py:13
  412.4 97.6 %all-to-all-start.6 = ((bf16[16,128,1024]{2,1,0:T(8,128)(2,1)}), bf16[16,128,1024]{2,1,0:T(8,128)(2,1)}, u32[]{:S(2)}, u32[]{:S(2)}) async-start(bf16[16,128,1024]{2,1,0:T(8,128)(2,1)} %bitcast.128), calls=%async_computation.6 | async-start | bytes 8388608 | tf_op jit(solution)/shard_map/all_to_all | solution.py:13
where the time goes:
time: 550 us; the launch traced here: 541 us
  local copies, waits for them, and re-layouts  170 us (31%)
  blocking collectives  149 us (27%)
  waiting for transfers between devices  139 us (25%)
  matrix products  43.1 us (8%)
  starting transfers between devices  24.6 us (4%)
  other arithmetic  13.8 us (3%)
    all_to_all x2, waiting for transfers between devices, to_time(): lax.all_to_all(field, 'freq', split_axis=0, concat_axis=1, tiled=True)  132 us
    unnamed x1, blocking collectives  88.9 us
    unnamed x24, local copies, waits for them, and re-layouts  79.9 us
    all_to_all x2, blocking collectives, forward(): lax.all_to_all(spectrum, 'freq', split_axis=0, concat_axis=2, tiled=True)  28.2 us
    another operation x6, local copies, waits for them, and re-layouts, convolve(): jnp.stack([out_r.astype(jnp.bfloat16), out_i.astype(jnp.bfloat16)], axis=1)  26.2 us
    all_to_all x4, local copies, waits for them, and re-layouts, convolve(): lax.all_to_all(stacked.reshape(nfreq_dev, 2, columns), 'freq', split_axis...  24.3 us
    all_gather x1, blocking collectives, local(): lax.all_gather(refl_scale, 'freq', axis=0, tiled=True)  18.6 us
    convert_element_type x2, local copies, waits for them, and re-layouts, local(): to_time(update_cols).astype(jnp.float32)  17.6 us
  transfers between devices with their start and end apart: 4, of which 3 were waited for; matrix products, arithmetic and copies ran while one was open for 10% of the time, Pallas kernels for 0%

commit v1 on v0

--- a/solution.py
+++ b/solution.py
@@ -3,6 +3,19 @@
 import jax.numpy as jnp
 from jax import lax
 from jax.sharding import PartitionSpec as P
+
+
+def ring_gather(x, axis, dim):
+    ways = lax.axis_size(axis)
+    up = [(d, (d + 1) % ways) for d in range(ways)]
+    down = [(d, (d - 1) % ways) for d in range(ways)]
+    earlier, later = ([x], [x])
+    for _ in range(ways // 2):
+        earlier.append(lax.ppermute(earlier[-1], axis, up))
+    for _ in range((ways - 1) // 2):
+        later.append(lax.ppermute(later[-1], axis, down))
+    line = jnp.concatenate([*earlier[::-1], *later[1:]], axis=dim)
+    return jnp.roll(line, (lax.axis_index(axis) - ways // 2) * x.shape[dim], axis=dim)
 
 
 def to_columns(field):
@@ -24,7 +37,7 @@
     first_col = lax.axis_index("freq") * width
     bins, scales = (
         lax.all_gather(freq_index, "freq", axis=0, tiled=True),
-        lax.all_gather(refl_scale, "freq", axis=0, tiled=True),
+        ring_gather(refl_scale, "freq", 0),
     )
     nblocks = scales.shape[1]
     times = jnp.arange(ntime, dtype=jnp.int32)

time: 550 us -> 572 us (1.040)
  starting transfers between devices: 24.6 us -> 49.5 us
  blocking collectives: 149 us -> 139 us
  waiting for transfers between devices: 139 us -> 145 us
    ppermute x0 -> x15, starting transfers between devices: none -> 25 us  [the longest x8 24.6 us: ring_gather(): earlier.append(lax.ppermute(earlier[-1], axis, up))]
    all_gather x1 -> x0, blocking collectives: 18.6 us -> none  [local(): lax.all_gather(refl_scale, 'freq', axis=0, tiled=True)]
    all_to_all x2, blocking collectives: 28.2 us -> 40 us  [forward(): lax.all_to_all(spectrum, 'freq', split_axis=0, concat_axis=2, tiled=True)]
    unnamed x24 -> x25, local copies, waits for them, and re-layouts: 79.9 us -> 80 us
  transfers between devices with their start and end apart: 4 -> 19, of which waited for: 3 -> 10; matrix products, arithmetic and copies ran while one was open for 10% -> 10% of each run, Pallas kernels for 0% -> 0%
where the time goes in v1:
time: 572 us; the launch traced here: 562 us
  local copies, waits for them, and re-layouts  170 us (30%)
  waiting for transfers between devices  145 us (25%)
  blocking collectives  139 us (24%)
  starting transfers between devices  49.5 us (9%)
  matrix products  43.3 us (8%)
  other arithmetic  13.8 us (2%)
    all_to_all x2, waiting for transfers between devices, to_time(): lax.all_to_all(field, 'freq', split_axis=0, concat_axis=1, tiled=True)  132 us
    unnamed x1, blocking collectives  86.1 us
    unnamed x25, local copies, waits for them, and re-layouts  80 us
    all_to_all x2, blocking collectives, forward(): lax.all_to_all(spectrum, 'freq', split_axis=0, concat_axis=2, tiled=True)  40 us
    another operation x6, local copies, waits for them, and re-layouts, convolve(): jnp.stack([out_r.astype(jnp.bfloat16), out_i.astype(jnp.bfloat16)], axis=1)  26.2 us
    ppermute x8, starting transfers between devices, ring_gather(): earlier.append(lax.ppermute(earlier[-1], axis, up))  24.6 us
    all_to_all x4, local copies, waits for them, and re-layouts, convolve(): lax.all_to_all(stacked.reshape(nfreq_dev, 2, columns), 'freq', split_axis...  24.3 us
    convert_element_type x2, local copies, waits for them, and re-layouts, local(): to_time(update_cols).astype(jnp.float32)  17.7 us
  transfers between devices with their start and end apart: 19, of which 10 were waited for; matrix products, arithmetic and copies ran while one was open for 10% of the time, Pallas kernels for 0%

profile of v1, /device:TPU:11, one launch (start us, length us, event | category | flops | bytes accessed | tf_op | source)
XLA Modules:
  0.0 562.1 jit_solution(8925516264566464042)
XLA Ops:
  0.6 7.9 %copy.55 = bf16[128,32,512]{0,2,1:T(8,128)(2,1)} copy(bf16[128,32,512]{2,1,0:T(8,128)(2,1)} %param.8) | data formatting | bytes 8388608 | tf_op args[3]
  8.5 6.7 %all-to-all-start = ((bf16[128,16,1024]{0,2,1:T(8,128)(2,1)}), bf16[128,16,1024]{0,2,1:T(8,128)(2,1)}, u32[]{:S(2)}, u32[]{:S(2)}) async-start(bf16[128,16,1024]{0,2,1:T(8,128)(2,1)} %bitcast.121), calls=%async_computation | async-start | bytes 8388608 | tf_op jit(solution)/shard_map/all_to_all | solution.py:22
  19.4 86.1 %all-reduce = s32[64]{0:T(128)S(1)} all-reduce(s32[64]{0:T(128)S(1)} %dynamic-update-slice), channel_id=1, replica_groups=mesh['groups'=2,'freq'=16] {'freq'}, use_global_device_ids=true, to_apply=%add | all-reduce | flops 64 | bytes 512
  105.6 3.3 collective-permute-start.1
  109.6 3.2 collective-permute-start.2
  133.6 6.4 %copy.56 = bf16[16,128,1024]{2,1,0:T(8,128)(2,1)} copy(bf16[16,128,1024]{1,2,0:T(8,128)(2,1)} %bitcast.2) | data formatting | bytes 8388608 | tf_op jit(solution)/shard_map/all_to_all | solution.py:22
  140.0 4.5 fusion.64
  147.4 27.0 %all_to_all.114 = bf16[64,2,1024]{2,1,0:T(2,128)(2,1)S(1)} all-to-all(bf16[64,2,1024]{2,1,0:T(2,128)(2,1)S(1)} %copy.61), channel_id=1, replica_groups=mesh['groups'=2,'freq'=16] {'freq'}, dimensions={0} | all-to-all | bytes 524288 | tf_op jit(solution)/shard_map/all_to_all | solution.py:67
  182.8 13.0 %copy.65 = bf16[4,2,16384]{0,1,2:T(2,128)(2,1)} copy(bf16[4,2,16384]{2,0,1:T(4,128)(2,1)S(1)} %pad_maximum_fusion.1) | data formatting | bytes 524288 | tf_op jit(solution)/shard_map/stack | solution.py:81
  195.8 16.8 %reshape.91 = bf16[16,2,4096]{2,1,0:T(2,128)(2,1)} reshape(bf16[16384,2,4]{2,1,0:T(2,128)(2,1)} %bitcast.117) | data formatting | bytes 524288
  212.6 6.1 %all-to-all-start.2 = ((bf16[16,2,4096]{2,1,0:T(2,128)(2,1)}), bf16[16,2,4096]{2,1,0:T(2,128)(2,1)S(1)}, u32[]{:S(2)}, u32[]{:S(2)}) async-start(bf16[16,2,4096]{2,1,0:T(2,128)(2,1)} %reshape.91), calls=%async_computation.2 | async-start | bytes 524288 | tf_op jit(solution)/shard_map/all_to_all | solution.py:82
  218.7 7.9 %all-to-all-done.2 = bf16[16,2,4096]{2,1,0:T(2,128)(2,1)S(1)} async-done(((bf16[16,2,4096]{2,1,0:T(2,128)(2,1)}), bf16[16,2,4096]{2,1,0:T(2,128)(2,1)S(1)}, u32[]{:S(2)}, u32[]{:S(2)}) %all-to-all-start.2) | async-done | bytes 262176 | tf_op jit(solution)/shard_map/all_to_all | solution.py:82
  226.6 19.0 %reshape.92 = bf16[16384,2,4]{2,1,0:T(2,128)(2,1)} reshape(bf16[16,2,4096]{2,1,0:T(2,128)(2,1)S(1)} %all-to-all-done.2) | data formatting | bytes 524288
  245.6 11.9 %copy.75 = bf16[4,2,16,1024]{3,2,1,0:T(8,128)(2,1)S(1)} copy(bf16[4,2,16,1024]{0,1,3,2:T(2,128)(2,1)} %bitcast.118) | data formatting | bytes 524288 | tf_op jit(solution)/shard_map/all_to_all | solution.py:82
  261.3 4.1 fusion
  270.8 13.0 %all_to_all.115 = bf16[64,2,1024]{2,1,0:T(2,128)(2,1)S(1)} all-to-all(bf16[64,2,1024]{2,1,0:T(2,128)(2,1)S(1)} %copy.69), channel_id=1, replica_groups=mesh['groups'=2,'freq'=16] {'freq'}, dimensions={0} | all-to-all | bytes 524288 | tf_op jit(solution)/shard_map/all_to_all | solution.py:67
  292.3 13.0 %copy.71 = bf16[4,2,16384]{0,1,2:T(2,128)(2,1)} copy(bf16[4,2,16384]{2,0,1:T(4,128)(2,1)S(1)} %pad_maximum_fusion.3) | data formatting | bytes 524288 | tf_op jit(solution)/shard_map/stack | solution.py:81
  305.3 16.2 %reshape.93 = bf16[16,2,4096]{2,1,0:T(2,128)(2,1)S(1)} reshape(bf16[16384,2,4]{2,1,0:T(2,128)(2,1)} %bitcast.119) | data formatting | bytes 524288
  321.5 12.8 %all_to_all.116 = bf16[16,2,4096]{2,1,0:T(2,128)(2,1)S(1)} all-to-all(bf16[16,2,4096]{2,1,0:T(2,128)(2,1)S(1)} %reshape.93), channel_id=1, replica_groups=mesh['groups'=2,'freq'=16] {'freq'}, dimensions={0} | all-to-all | bytes 524288 | tf_op jit(solution)/shard_map/all_to_all | solution.py:82
  334.3 6.5 %all-to-all-start.3 = ((bf16[16,128,1024]{2,1,0:T(8,128)(2,1)}), bf16[16,128,1024]{2,1,0:T(8,128)(2,1)}, u32[]{:S(2)}, u32[]{:S(2)}) async-start(bf16[16,128,1024]{2,1,0:T(8,128)(2,1)} %bitcast.122), calls=%async_computation.3 | async-start | bytes 8388608 | tf_op jit(solution)/shard_map/all_to_all | solution.py:26
  340.8 19.1 %reshape.94 = bf16[16384,2,4]{2,1,0:T(2,128)(2,1)} reshape(bf16[16,2,4096]{2,1,0:T(2,128)(2,1)S(1)} %all_to_all.116) | data formatting | bytes 524288
  359.8 11.9 %copy.76 = bf16[4,2,16,1024]{3,2,1,0:T(8,128)(2,1)S(1)} copy(bf16[4,2,16,1024]{0,1,3,2:T(2,128)(2,1)} %bitcast.120) | data formatting | bytes 524288 | tf_op jit(solution)/shard_map/all_to_all | solution.py:82
  375.5 4.9 fusion.1
  380.5 52.8 %all-to-all-done.3 = bf16[16,128,1024]{2,1,0:T(8,128)(2,1)} async-done(((bf16[16,128,1024]{2,1,0:T(8,128)(2,1)}), bf16[16,128,1024]{2,1,0:T(8,128)(2,1)}, u32[]{:S(2)}, u32[]{:S(2)}) %all-to-all-start.3) | async-done | bytes 4194336 | tf_op jit(solution)/shard_map/all_to_all | solution.py:26
  433.3 5.2 all-to-all-start.6
  438.5 6.5 %copy.68 = bf16[128,16,1024]{2,1,0:T(8,128)(2,1)} copy(bf16[128,16,1024]{2,0,1:T(8,128)(2,1)} %bitcast.16) | data formatting | bytes 8388608 | tf_op jit(solution)/shard_map/all_to_all | solution.py:26
  445.0 7.1 %reshape.83 = bf16[128,32,512]{2,1,0:T(8,128)(2,1)} reshape(bf16[128,16,1024]{2,1,0:T(8,128)(2,1)} %copy.68) | data formatting | bytes 8388608 | tf_op jit(solution)/shard_map/reshape | solution.py:100
  452.1 78.7 %all-to-all-done.6 = bf16[16,128,1024]{2,1,0:T(8,128)(2,1)} async-done(((bf16[16,128,1024]{2,1,0:T(8,128)(2,1)}), bf16[16,128,1024]{2,1,0:T(8,128)(2,1)}, u32[]{:S(2)}, u32[]{:S(2)}) %all-to-all-start.6) | async-done | bytes 4194336 | tf_op jit(solution)/shard_map/all_to_all | solution.py:26
  530.8 3.2 convert_bitcast_fusion
  534.1 8.3 %copy.74 = f32[128,16,1024]{2,1,0:T(8,128)} copy(f32[128,16,1024]{2,0,1:T(8,128)S(1)} %convert_bitcast_fusion) | data formatting | bytes 16777216 | tf_op jit(solution)/shard_map/convert_element_type | solution.py:99
  542.3 9.4 %reshape.85 = f32[128,32,512]{2,1,0:T(8,128)} reshape(f32[128,16,1024]{2,1,0:T(8,128)} %copy.74) | data formatting | bytes 16777216 | tf_op jit(solution)/shard_map/convert_element_type | solution.py:99
  551.7 10.2 %convert_add_fusion = f32[128,32,512]{2,1,0:T(8,128)} fusion(f32[128,32,512]{2,1,0:T(8,128)} %reshape.85, bf16[128,32,512]{2,1,0:T(8,128)(2,1)} %param.8), kind=kLoop, calls=%fused_computation.5 | loop fusion | flops 4194304 | bytes 20971520 | tf_op jit(solution)/shard_map/add | solution.py:99
  (84 shorter events, 57.6 us)
Async XLA Ops:
  8.5 6.7 %copy-start.4 = (f32[4,4]{1,0:T(4,128)S(1)}, f32[4,4]{1,0:T(4,128)}, u32[]{:S(2)}) copy-start(f32[4,4]{1,0:T(4,128)} %param.6) | copy-start | bytes 196
  8.5 9.4 %copy-start.7 = (u32[32]{0:T(128)S(1)}, u32[32]{0:T(128)}, u32[]{:S(2)}) copy-start(u32[32]{0:T(128)} %constant.94) | copy-start | bytes 388
  8.5 10.7 %copy-start.6 = (s32[4]{0:T(128)S(1)}, s32[4]{0:T(128)}, u32[]{:S(2)}) copy-start(s32[4]{0:T(128)} %param.7) | copy-start | bytes 52
  8.5 125.1 %all-to-all-start = ((bf16[128,16,1024]{0,2,1:T(8,128)(2,1)}), bf16[128,16,1024]{0,2,1:T(8,128)(2,1)}, u32[]{:S(2)}, u32[]{:S(2)}) async-start(bf16[128,16,1024]{0,2,1:T(8,128)(2,1)} %bitcast.121), calls=%async_computation | async-start | bytes 8388608 | tf_op jit(solution)/shard_map/all_to_all | solution.py:22
  15.3 93.6 %collective-permute-start.8 = (f32[4,4]{0,1:T(4,128)S(1)}, f32[4,4]{0,1:T(4,128)S(1)}, u32[]{:S(2)}, u32[]{:S(2)}) collective-permute-start(f32[4,4]{0,1:T(4,128)S(1)} %copy.57), channel_id=1, source_target_pairs={{0,15},{1,0},{2,1},{3,2},{4,3},{5,4},{6,5},{7,6},{8,7},{9,8},{10,9... | collective-permute-start | bytes 200 | tf_op jit(solution)/shard_map/ppermute | solution.py:16
  15.7 90.0 %collective-permute-start = (f32[4,4]{0,1:T(4,128)S(1)}, f32[4,4]{0,1:T(4,128)S(1)}, u32[]{:S(2)}, u32[]{:S(2)}) collective-permute-start(f32[4,4]{0,1:T(4,128)S(1)} %copy.57), channel_id=1, source_target_pairs={{0,1},{1,2},{2,3},{3,4},{4,5},{5,6},{6,7},{7,8},{8,9},{9,10},{10,1... | collective-permute-start | bytes 200 | tf_op jit(solution)/shard_map/ppermute | solution.py:14
  105.6 4.0 collective-permute-start.1
  108.9 3.9 collective-permute-start.9
  109.6 3.9 collective-permute-start.2
  112.8 3.9 collective-permute-start.10
  113.5 3.9 collective-permute-start.3
  116.7 3.9 collective-permute-start.11
  117.4 3.9 collective-permute-start.4
  120.6 3.9 collective-permute-start.12
  121.3 3.9 collective-permute-start.5
  124.5 3.9 collective-permute-start.13
  125.3 3.9 collective-permute-start.6
  128.4 3.9 collective-permute-start.14
  129.2 3.9 collective-permute-start.7
  140.0 4.5 copy-start.3
  174.6 4.8 copy-start
  212.6 14.0 %all-to-all-start.2 = ((bf16[16,2,4096]{2,1,0:T(2,128)(2,1)}), bf16[16,2,4096]{2,1,0:T(2,128)(2,1)S(1)}, u32[]{:S(2)}, u32[]{:S(2)}) async-start(bf16[16,2,4096]{2,1,0:T(2,128)(2,1)} %reshape.91), calls=%async_computation.2 | async-start | bytes 524288 | tf_op jit(solution)/shard_map/all_to_all | solution.py:82
  258.2 3.1 copy-start.5
  265.4 5.1 copy-start.2
  284.1 4.8 copy-start.1
  334.3 99.0 %all-to-all-start.3 = ((bf16[16,128,1024]{2,1,0:T(8,128)(2,1)}), bf16[16,128,1024]{2,1,0:T(8,128)(2,1)}, u32[]{:S(2)}, u32[]{:S(2)}) async-start(bf16[16,128,1024]{2,1,0:T(8,128)(2,1)} %bitcast.122), calls=%async_computation.3 | async-start | bytes 8388608 | tf_op jit(solution)/shard_map/all_to_all | solution.py:26
  433.3 97.6 %all-to-all-start.6 = ((bf16[16,128,1024]{2,1,0:T(8,128)(2,1)}), bf16[16,128,1024]{2,1,0:T(8,128)(2,1)}, u32[]{:S(2)}, u32[]{:S(2)}) async-start(bf16[16,128,1024]{2,1,0:T(8,128)(2,1)} %bitcast.123), calls=%async_computation.6 | async-start | bytes 8388608 | tf_op jit(solution)/shard_map/all_to_all | solution.py:26
